TPU v7x, 32 devices: a whole 2x2x4 slice. The times are simulated.
32 devices in a mesh: band: 2 (over core), plane: 16 (over z, y, x).
Axes of the slice: x: 2, y: 2, z: 4, core: 2. Of those that a mesh axis runs over, the one named last changes fastest.
Arguments:
- bands: float32 [8, 128, 128, 128], P('band', 'plane'), may hold values from -6 to 6
- plan: int32 [2], replicated, may hold values from 0 to 7
Outputs:
- exchange_part: float32 [8, 128, 128, 128], P('band', 'plane')
All inputs are finite; a program needn't handle non-finite values.
Results may differ from a plain program's by a relative error of at most 0.00011.
Values sent between devices are 32-bit elements; how exact they have to be, the bound alone decides.
No kernel may reach another device: no remote copies, remote signals or barrier semaphores. Data moves between devices by JAX's collectives and lax.ppermute only.
A program may use at most 64 MiB of HBM per device.

v0:
```python
import math
import jax
import jax.numpy as jnp
from jax import lax
from jax.sharding import PartitionSpec as P

screening = 0.1
highest = lax.Precision.HIGHEST


def spread(value, axis, source):
    kept = jnp.where(lax.axis_index(axis) == source, value, 0).astype(value.dtype)
    return lax.psum(kept, axis)


def tables(points, retained):
    lowest = jnp.arange(retained // 2, dtype=jnp.int32)
    spectral = jnp.concatenate([lowest, lowest - retained // 2])
    where_grid = jnp.arange(points, dtype=jnp.int32)
    phases = spectral[:, None] * where_grid[None, :] % points
    angles = phases.astype(jnp.float32) * (2.0 * math.pi / points)
    return (jnp.cos(angles), jnp.sin(angles), spectral)


def coulomb(spectral, points):
    squared = (
        spectral[:, None, None] ** 2 + spectral[None, :, None] ** 2 + spectral[None, None, :] ** 2
    )
    spacing = 2.0 * math.pi / points
    values = 1.0 / (spacing * spacing * squared.astype(jnp.float32) + screening * screening)
    return jnp.where(squared < (points // 4) ** 2, values, 0.0)


def along_last(values, table):
    return jnp.einsum("bxyz,kz->bxyk", values, table, precision=highest)


def back_last(values, table):
    return jnp.einsum("bxyk,kz->bxyz", values, table, precision=highest)


def along_rows(values, table):
    return jnp.einsum("bxyk,jy->bxjk", values, table, precision=highest)


def back_rows(values, table):
    return jnp.einsum("bxjk,jy->bxyk", values, table, precision=highest)


def along_planes(values, table):
    return jnp.einsum("bxsc,kx->bksc", values, table, precision=highest)


def back_planes(values, table):
    return jnp.einsum("bksc,kx->bxsc", values, table, precision=highest)


def per_device(bands, plan):
    local_count, planes, points = (bands.shape[0], bands.shape[1], bands.shape[2])
    plane_count = lax.axis_size("plane")
    cos_table, sin_table, spectral = tables(points, points)
    share = points // plane_count
    kernel_full = coulomb(spectral, points).reshape(points, points * points)
    kernel_mine = lax.dynamic_slice_in_dim(
        kernel_full, lax.axis_index("plane") * (share * points), share * points, 1
    )
    kernel_mine = kernel_mine[:, None, :]
    scale_back = 1.0 / float(points) ** 3
    accumulated = jnp.zeros(bands.shape, jnp.float32)
    for turn_index in range(plan.shape[0]):
        chosen = plan[turn_index]
        own_band = lax.dynamic_index_in_dim(bands, chosen % local_count, 0, keepdims=False)
        partner = spread(own_band, "band", chosen // local_count)
        density = partner[None] * bands
        potentials_real_part = along_last(density, cos_table)
        potentials_imag_part = -along_last(density, sin_table)
        row_real = along_rows(potentials_real_part, cos_table) + along_rows(
            potentials_imag_part, sin_table
        )
        row_imag = along_rows(potentials_imag_part, cos_table) - along_rows(
            potentials_real_part, sin_table
        )
        items = density.shape[0]
        shaped = (items, planes, plane_count, share * points)
        real_part = lax.all_to_all(
            row_real.reshape(shaped), "plane", split_axis=2, concat_axis=1, tiled=True
        )
        imag_part = lax.all_to_all(
            row_imag.reshape(shaped), "plane", split_axis=2, concat_axis=1, tiled=True
        )
        fwd_real = along_planes(real_part, cos_table) + along_planes(imag_part, sin_table)
        fwd_imag = along_planes(imag_part, cos_table) - along_planes(real_part, sin_table)
        fwd_real = fwd_real * kernel_mine
        fwd_imag = fwd_imag * kernel_mine
        back_real = back_planes(fwd_real, cos_table) - back_planes(fwd_imag, sin_table)
        back_imag = back_planes(fwd_real, sin_table) + back_planes(fwd_imag, cos_table)
        out_real = lax.all_to_all(back_real, "plane", split_axis=1, concat_axis=2, tiled=True)
        out_imag = lax.all_to_all(back_imag, "plane", split_axis=1, concat_axis=2, tiled=True)
        out_real = out_real.reshape(items, planes, points, points)
        out_imag = out_imag.reshape(items, planes, points, points)
        col_real = back_rows(out_real, cos_table) - back_rows(out_imag, sin_table)
        col_imag = back_rows(out_real, sin_table) + back_rows(out_imag, cos_table)
        first_back = (back_last(col_real, cos_table) - back_last(col_imag, sin_table)) * scale_back
        accumulated = accumulated - partner[None] * first_back
    return accumulated


def solution(mesh):
    in_specs = (P("band", "plane", None, None), P())
    out_specs = P("band", "plane", None, None)
    return jax.shard_map(
        per_device, mesh=mesh, in_specs=in_specs, out_specs=out_specs, check_vma=False
    )
```

profile of v0, /device:TPU:12, one launch (start us, length us, event | category | flops | bytes accessed | tf_op | source)
XLA Modules:
  0.0 505.0 jit_solution(16058967309255782225)
XLA Ops:
  15.7 21.1 %all-reduce.3.cloned.1.call-done = (f32[8,128,128]{2,1,0:T(8,128)}, f32[8,128,128]{2,1,0:T(8,128)}) async-done(((f32[8,128,128]{2,1,0:T(8,128)}, f32[8,128,128]{2,1,0:T(8,128)}), (f32[8,128,128]{2,1,0:T(8,128)}, f32[8,128,128]{2,1,0:T(8,128)})) %all-reduce.3.cloned.1.call-update) | async-done | bytes 1048592 | tf_op jit(solution)/shard_map/psum | solution.py:13
  54.9 7.3 %all-to-all-start.1 = ((f32[4,8,16,1024]{3,1,0,2:T(8,128)}), f32[4,8,16,1024]{3,1,0,2:T(8,128)}, u32[]{:S(2)}, u32[]{:S(2)}) async-start(f32[4,8,16,1024]{3,1,0,2:T(8,128)} %copy.33), calls=%async_computation.1 | async-start | bytes 4194304 | tf_op jit(solution)/shard_map/all_to_all | solution.py:88
  72.4 4.2 copy.31
  76.6 33.9 %all-to-all-done.1 = f32[4,8,16,1024]{3,1,0,2:T(8,128)} async-done(((f32[4,8,16,1024]{3,1,0,2:T(8,128)}), f32[4,8,16,1024]{3,1,0,2:T(8,128)}, u32[]{:S(2)}, u32[]{:S(2)}) %all-to-all-start.1) | async-done | bytes 2097184 | tf_op jit(solution)/shard_map/all_to_all | solution.py:88
  110.5 5.4 %all-to-all-start = ((f32[4,8,16,1024]{3,1,0,2:T(8,128)}), f32[4,8,16,1024]{3,1,0,2:T(8,128)}, u32[]{:S(2)}, u32[]{:S(2)}) async-start(f32[4,8,16,1024]{3,1,0,2:T(8,128)} %copy.31), calls=%async_computation | async-start | bytes 4194304 | tf_op jit(solution)/shard_map/all_to_all | solution.py:85
  132.8 30.8 %all-to-all-done = f32[4,8,16,1024]{3,1,0,2:T(8,128)} async-done(((f32[4,8,16,1024]{3,1,0,2:T(8,128)}), f32[4,8,16,1024]{3,1,0,2:T(8,128)}, u32[]{:S(2)}, u32[]{:S(2)}) %all-to-all-start) | async-done | bytes 2097184 | tf_op jit(solution)/shard_map/all_to_all | solution.py:85
  163.6 5.2 %all-to-all-start.5 = ((f32[4,8,16,1024]{3,1,0,2:T(8,128)}), f32[4,8,16,1024]{3,1,0,2:T(8,128)}, u32[]{:S(2)}, u32[]{:S(2)}) async-start(f32[4,8,16,1024]{3,1,0,2:T(8,128)} %copy.49), calls=%async_computation.5 | async-start | bytes 4194304 | tf_op jit(solution)/shard_map/all_to_all | solution.py:88
  174.8 4.2 copy.47
  179.0 37.4 %all-to-all-done.5 = f32[4,8,16,1024]{3,1,0,2:T(8,128)} async-done(((f32[4,8,16,1024]{3,1,0,2:T(8,128)}), f32[4,8,16,1024]{3,1,0,2:T(8,128)}, u32[]{:S(2)}, u32[]{:S(2)}) %all-to-all-start.5) | async-done | bytes 2097184 | tf_op jit(solution)/shard_map/all_to_all | solution.py:88
  216.4 4.6 all-to-all-start.4
  223.7 9.8 %copy.143 = s32[16,8,128,128]{3,1,2,0:T(8,128)} copy(s32[16,8,128,128]{3,2,1,0:T(8,128)S(1)} %bitcast.314) | data formatting | bytes 16777216
  257.9 11.0 %all-to-all-done.4 = f32[4,8,16,1024]{3,1,0,2:T(8,128)} async-done(((f32[4,8,16,1024]{3,1,0,2:T(8,128)}), f32[4,8,16,1024]{3,1,0,2:T(8,128)}, u32[]{:S(2)}, u32[]{:S(2)}) %all-to-all-start.4) | async-done | bytes 2097184 | tf_op jit(solution)/shard_map/all_to_all | solution.py:85
  268.8 4.5 all-to-all-start.2
  282.1 38.9 %all-to-all-done.2 = f32[4,128,1,1024]{3,0,2,1:T(4,128)} async-done(((f32[4,128,1,1024]{3,0,2,1:T(4,128)}), f32[4,128,1,1024]{3,0,2,1:T(4,128)}, u32[]{:S(2)}, u32[]{:S(2)}) %all-to-all-start.2) | async-done | bytes 2097184 | tf_op jit(solution)/shard_map/all_to_all | solution.py:97
  321.0 4.6 all-to-all-start.3
  348.8 24.1 %all-to-all-done.3 = f32[4,128,1,1024]{3,0,2,1:T(4,128)} async-done(((f32[4,128,1,1024]{3,0,2,1:T(4,128)}), f32[4,128,1,1024]{3,0,2,1:T(4,128)}, u32[]{:S(2)}, u32[]{:S(2)}) %all-to-all-start.3) | async-done | bytes 2097184 | tf_op jit(solution)/shard_map/all_to_all | solution.py:98
  372.9 4.6 all-to-all-start.7
  386.3 38.5 %all-to-all-done.7 = f32[4,128,1,1024]{3,0,2,1:T(4,128)} async-done(((f32[4,128,1,1024]{3,0,2,1:T(4,128)}), f32[4,128,1,1024]{3,0,2,1:T(4,128)}, u32[]{:S(2)}, u32[]{:S(2)}) %all-to-all-start.7) | async-done | bytes 2097184 | tf_op jit(solution)/shard_map/all_to_all | solution.py:98
  424.8 4.7 all-to-all-start.6
  430.4 4.1 copy.147
  436.2 4.1 copy.146
  443.1 4.2 copy.144
  450.1 5.3 %fusion.139 = f32[128,4,8,128]{3,0,2,1:T(8,128)} fusion(f32[4,8,128,128]{3,2,1,0:T(8,128)} %reshape.182, s32[128]{0:T(128)S(1)} %get-tuple-element.8), kind=kOutput, calls=%fused_computation.140 | convolution fusion | flops 805535744 | bytes 4194816 | tf_op jit(solution)/shard_map/bxjk,jy->bxyk/dot_general | solution.py:47
  476.7 4.1 copy.145
  (110 shorter events, 168.6 us)
Async XLA Ops:
  6.5 30.3 %copy-start = (f32[4,8,128,128]{3,2,1,0:T(8,128)S(1)}, f32[4,8,128,128]{3,2,1,0:T(8,128)}, u32[]{:S(2)}) copy-start(f32[4,8,128,128]{3,2,1,0:T(8,128)} %param.2) | copy-start | bytes 6291460
  6.5 30.3 %all-reduce.3.cloned.1.call-start = ((), (), s32[]{:S(2)}) async-start(), calls=%async_computation.8 | async-start | bytes 2097152 | tf_op jit(solution)/shard_map/psum | solution.py:13
  36.8 3.3 copy-start.19
  42.3 2.2 copy-start.3
  54.9 55.6 %all-to-all-start.1 = ((f32[4,8,16,1024]{3,1,0,2:T(8,128)}), f32[4,8,16,1024]{3,1,0,2:T(8,128)}, u32[]{:S(2)}, u32[]{:S(2)}) async-start(f32[4,8,16,1024]{3,1,0,2:T(8,128)} %copy.33), calls=%async_computation.1 | async-start | bytes 4194304 | tf_op jit(solution)/shard_map/all_to_all | solution.py:88
  62.2 3.9 copy-start.4
  76.6 39.2 %copy-start.18 = (f32[8,128,128]{2,1,0:T(8,128)S(1)}, f32[8,128,128]{2,1,0:T(8,128)}, u32[]{:S(2)}) copy-start(f32[8,128,128]{2,1,0:T(8,128)} %get-tuple-element.5) | copy-start | bytes 1572868
  110.5 53.2 %all-to-all-start = ((f32[4,8,16,1024]{3,1,0,2:T(8,128)}), f32[4,8,16,1024]{3,1,0,2:T(8,128)}, u32[]{:S(2)}, u32[]{:S(2)}) async-start(f32[4,8,16,1024]{3,1,0,2:T(8,128)} %copy.31), calls=%async_computation | async-start | bytes 4194304 | tf_op jit(solution)/shard_map/all_to_all | solution.py:85
  132.8 36.1 %copy-start.6 = (f32[4,8,128,128]{3,2,1,0:T(8,128)S(1)}, f32[4,8,128,128]{3,2,1,0:T(8,128)}, u32[]{:S(2)}) copy-start(f32[4,8,128,128]{3,2,1,0:T(8,128)} %copy-done.5) | copy-start | bytes 6291460
  163.6 52.7 %all-to-all-start.5 = ((f32[4,8,16,1024]{3,1,0,2:T(8,128)}), f32[4,8,16,1024]{3,1,0,2:T(8,128)}, u32[]{:S(2)}, u32[]{:S(2)}) async-start(f32[4,8,16,1024]{3,1,0,2:T(8,128)} %copy.49), calls=%async_computation.5 | async-start | bytes 4194304 | tf_op jit(solution)/shard_map/all_to_all | solution.py:88
  168.9 2.2 copy-start.2
  216.4 52.4 %all-to-all-start.4 = ((f32[4,8,16,1024]{3,1,0,2:T(8,128)}), f32[4,8,16,1024]{3,1,0,2:T(8,128)}, u32[]{:S(2)}, u32[]{:S(2)}) async-start(f32[4,8,16,1024]{3,1,0,2:T(8,128)} %copy.47), calls=%async_computation.4 | async-start | bytes 4194304 | tf_op jit(solution)/shard_map/all_to_all | solution.py:85
  242.5 2.7 copy-start.9
  268.8 52.1 %all-to-all-start.2 = ((f32[4,128,1,1024]{3,0,2,1:T(4,128)}), f32[4,128,1,1024]{3,0,2,1:T(4,128)}, u32[]{:S(2)}, u32[]{:S(2)}) async-start(f32[4,128,1,1024]{3,0,2,1:T(4,128)} %copy.37), calls=%async_computation.2 | async-start | bytes 4194304 | tf_op jit(solution)/shard_map/all_to_all | solution.py:97
  321.0 51.9 %all-to-all-start.3 = ((f32[4,128,1,1024]{3,0,2,1:T(4,128)}), f32[4,128,1,1024]{3,0,2,1:T(4,128)}, u32[]{:S(2)}, u32[]{:S(2)}) async-start(f32[4,128,1,1024]{3,0,2,1:T(4,128)} %copy.42), calls=%async_computation.3 | async-start | bytes 4194304 | tf_op jit(solution)/shard_map/all_to_all | solution.py:98
  333.4 2.2 copy-start.8
  372.9 51.8 %all-to-all-start.7 = ((f32[4,128,1,1024]{3,0,2,1:T(4,128)}), f32[4,128,1,1024]{3,0,2,1:T(4,128)}, u32[]{:S(2)}, u32[]{:S(2)}) async-start(f32[4,128,1,1024]{3,0,2,1:T(4,128)} %copy.58), calls=%async_computation.7 | async-start | bytes 4194304 | tf_op jit(solution)/shard_map/all_to_all | solution.py:98
  386.3 43.2 %copy-start.20 = (f32[8,128,128]{2,1,0:T(8,128)S(1)}, f32[8,128,128]{2,1,0:T(8,128)}, u32[]{:S(2)}) copy-start(f32[8,128,128]{2,1,0:T(8,128)} %get-tuple-element.6) | copy-start | bytes 1572868
  424.8 51.9 %all-to-all-start.6 = ((f32[4,128,1,1024]{3,0,2,1:T(4,128)}), f32[4,128,1,1024]{3,0,2,1:T(4,128)}, u32[]{:S(2)}, u32[]{:S(2)}) async-start(f32[4,128,1,1024]{3,0,2,1:T(4,128)} %copy.53), calls=%async_computation.6 | async-start | bytes 4194304 | tf_op jit(solution)/shard_map/all_to_all | solution.py:97
  450.1 5.3 %copy-start.11 = (f32[4,8,128,128]{3,2,1,0:T(8,128)S(1)}, f32[4,8,128,128]{3,2,1,0:T(8,128)}, u32[]{:S(2)}) copy-start(f32[4,8,128,128]{3,2,1,0:T(8,128)} %reshape.182) | copy-start | bytes 6291460
  462.6 3.6 copy-start.10
  485.0 2.3 copy-start.13
  485.0 2.3 copy-start.16
  487.2 2.2 copy-start.14
  (7 other events, 13.6 us)
Sparse Core Ops, SparseCore 0:
  15.8 21.0 all-reduce.2
where the time goes:
time: 514 us; the launch traced here: 505 us
  waiting for transfers between devices  239 us (46%)
  matrix products  123 us (24%)
  local copies, waits for them, and re-layouts  78.2 us (15%)
  starting transfers between devices  40.9 us (8%)
  between operations  19.7 us (4%)
    all_to_all x2, waiting for transfers between devices, per_device(): lax.all_to_all(row_imag.reshape(shaped), 'plane', split_axis=2, concat_ax...  71.3 us
    all_to_all x2, waiting for transfers between devices, per_device(): lax.all_to_all(back_imag, 'plane', split_axis=1, concat_axis=2, tiled=True)  62.6 us
    all_to_all x2, waiting for transfers between devices, per_device(): lax.all_to_all(back_real, 'plane', split_axis=1, concat_axis=2, tiled=True)  42.3 us
    all_to_all x2, waiting for transfers between devices, per_device(): lax.all_to_all(row_real.reshape(shaped), 'plane', split_axis=2, concat_ax...  41.8 us
    dot_general x8, matrix products, along_planes(): return jnp.einsum('bxsc,kx->bksc', values, table, precision=highest)  31.1 us
    dot_general x8, matrix products, back_rows(): return jnp.einsum('bxjk,jy->bxyk', values, table, precision=highest)  27.6 us
    dot_general x8, matrix products, back_planes(): return jnp.einsum('bksc,kx->bxsc', values, table, precision=highest)  21.9 us
    dot_general x8, matrix products, along_rows(): return jnp.einsum('bxyk,jy->bxjk', values, table, precision=highest)  21.9 us
  transfers between devices with their start and end apart: 9, of which 9 were waited for; matrix products, arithmetic and copies ran while one was open for 32% of the time, Pallas kernels for 0%

commit v1 on v0

--- a/solution.py
+++ b/solution.py
@@ -8,9 +8,13 @@
 highest = lax.Precision.HIGHEST
 
 
+def pack_block_for(x_in, net_axis):
+    return jnp.sum(lax.all_gather(x_in, axis_name=net_axis), axis=0)
+
+
 def spread(value, axis, source):
     kept = jnp.where(lax.axis_index(axis) == source, value, 0).astype(value.dtype)
-    return lax.psum(kept, axis)
+    return pack_block_for(kept, axis)
 
 
 def tables(points, retained):

time: 514 us -> 504 us (0.981)
  waiting for transfers between devices: 239 us -> 229 us
    all_gather x0 -> x2, waiting for transfers between devices: none -> 22.3 us  [pack_block_for(): return jnp.sum(lax.all_gather(x_in, axis_name=net_axis), axis=0)]
    psum x1 -> x0, waiting for transfers between devices: 21.1 us -> none  [spread(): return lax.psum(kept, axis)]
    all_to_all x2, waiting for transfers between devices: 62.6 us -> 77.4 us  [per_device(): lax.all_to_all(back_imag, 'plane', split_axis=1, concat_axis=2, tiled=True)]
    all_to_all x2, waiting for transfers between devices: 41.8 us -> 27.9 us  [per_device(): lax.all_to_all(row_real.reshape(shaped), 'plane', split_axis=2, concat_ax...]
    all_to_all x2, waiting for transfers between devices: 42.3 us -> 29.1 us  [per_device(): lax.all_to_all(back_real, 'plane', split_axis=1, concat_axis=2, tiled=True)]
    unnamed x45 -> x43, local copies, waits for them, and re-layouts: 12.6 us -> 12.6 us
  transfers between devices with their start and end apart: 9 -> 10, of which waited for: 9 -> 10; matrix products, arithmetic and copies ran while one was open for 32% -> 32% of each run, Pallas kernels for 0% -> 0%
where the time goes in v1:
time: 504 us; the launch traced here: 494 us
  waiting for transfers between devices  229 us (45%)
  matrix products  120 us (24%)
  local copies, waits for them, and re-layouts  78.3 us (16%)
  starting transfers between devices  41 us (8%)
  between operations  19.6 us (4%)
  other arithmetic  7.31 us (1%)
    all_to_all x2, waiting for transfers between devices, per_device(): lax.all_to_all(back_imag, 'plane', split_axis=1, concat_axis=2, tiled=True)  77.4 us
    all_to_all x2, waiting for transfers between devices, per_device(): lax.all_to_all(row_imag.reshape(shaped), 'plane', split_axis=2, concat_ax...  71.3 us
    dot_general x8, matrix products, along_planes(): return jnp.einsum('bxsc,kx->bksc', values, table, precision=highest)  30.9 us
    all_to_all x2, waiting for transfers between devices, per_device(): lax.all_to_all(back_real, 'plane', split_axis=1, concat_axis=2, tiled=True)  29.1 us
    all_to_all x2, waiting for transfers between devices, per_device(): lax.all_to_all(row_real.reshape(shaped), 'plane', split_axis=2, concat_ax...  27.9 us
    dot_general x8, matrix products, back_rows(): return jnp.einsum('bxjk,jy->bxyk', values, table, precision=highest)  25.9 us
    all_gather x2, waiting for transfers between devices, pack_block_for(): return jnp.sum(lax.all_gather(x_in, axis_name=net_axis), axis=0)  22.3 us
    dot_general x8, matrix products, back_planes(): return jnp.einsum('bksc,kx->bxsc', values, table, precision=highest)  21.9 us
  transfers between devices with their start and end apart: 10, of which 10 were waited for; matrix products, arithmetic and copies ran while one was open for 32% of the time, Pallas kernels for 0%

profile of v1, /device:TPU:12, one launch (start us, length us, event | category | flops | bytes accessed | tf_op | source)
XLA Modules:
  0.0 494.5 jit_solution(18365692164600785927)
XLA Ops:
  15.6 10.5 %all-gather.3.cloned.1.call-done = f32[2,8,128,128]{3,2,1,0:T(8,128)} async-done(((f32[1,8,128,128]{3,2,1,0:T(8,128)}), f32[2,8,128,128]{3,2,1,0:T(8,128)}) %all-gather.3.cloned.1.call-update) | async-done | bytes 1048592 | tf_op jit(solution)/shard_map/all_gather | solution.py:12
  44.3 7.3 %all-to-all-start.1 = ((f32[4,8,16,1024]{3,1,0,2:T(8,128)}), f32[4,8,16,1024]{3,1,0,2:T(8,128)}, u32[]{:S(2)}, u32[]{:S(2)}) async-start(f32[4,8,16,1024]{3,1,0,2:T(8,128)} %copy.33), calls=%async_computation.1 | async-start | bytes 4194304 | tf_op jit(solution)/shard_map/all_to_all | solution.py:92
  61.9 4.2 copy.31
  66.0 33.9 %all-to-all-done.1 = f32[4,8,16,1024]{3,1,0,2:T(8,128)} async-done(((f32[4,8,16,1024]{3,1,0,2:T(8,128)}), f32[4,8,16,1024]{3,1,0,2:T(8,128)}, u32[]{:S(2)}, u32[]{:S(2)}) %all-to-all-start.1) | async-done | bytes 2097184 | tf_op jit(solution)/shard_map/all_to_all | solution.py:92
  99.9 5.4 %all-to-all-start = ((f32[4,8,16,1024]{3,1,0,2:T(8,128)}), f32[4,8,16,1024]{3,1,0,2:T(8,128)}, u32[]{:S(2)}, u32[]{:S(2)}) async-start(f32[4,8,16,1024]{3,1,0,2:T(8,128)} %copy.31), calls=%async_computation | async-start | bytes 4194304 | tf_op jit(solution)/shard_map/all_to_all | solution.py:89
  106.1 11.8 %all-gather.5.cloned.1.call-done = f32[2,8,128,128]{3,2,1,0:T(8,128)} async-done(((f32[1,8,128,128]{3,2,1,0:T(8,128)}), f32[2,8,128,128]{3,2,1,0:T(8,128)}) %all-gather.5.cloned.1.call-update) | async-done | bytes 1048592 | tf_op jit(solution)/shard_map/all_gather | solution.py:12
  136.3 16.9 %all-to-all-done = f32[4,8,16,1024]{3,1,0,2:T(8,128)} async-done(((f32[4,8,16,1024]{3,1,0,2:T(8,128)}), f32[4,8,16,1024]{3,1,0,2:T(8,128)}, u32[]{:S(2)}, u32[]{:S(2)}) %all-to-all-start) | async-done | bytes 2097184 | tf_op jit(solution)/shard_map/all_to_all | solution.py:89
  153.2 5.2 %all-to-all-start.5 = ((f32[4,8,16,1024]{3,1,0,2:T(8,128)}), f32[4,8,16,1024]{3,1,0,2:T(8,128)}, u32[]{:S(2)}, u32[]{:S(2)}) async-start(f32[4,8,16,1024]{3,1,0,2:T(8,128)} %copy.49), calls=%async_computation.5 | async-start | bytes 4194304 | tf_op jit(solution)/shard_map/all_to_all | solution.py:92
  164.4 4.2 copy.47
  168.5 37.4 %all-to-all-done.5 = f32[4,8,16,1024]{3,1,0,2:T(8,128)} async-done(((f32[4,8,16,1024]{3,1,0,2:T(8,128)}), f32[4,8,16,1024]{3,1,0,2:T(8,128)}, u32[]{:S(2)}, u32[]{:S(2)}) %all-to-all-start.5) | async-done | bytes 2097184 | tf_op jit(solution)/shard_map/all_to_all | solution.py:92
  205.9 4.6 all-to-all-start.4
  213.3 9.8 %copy.143 = s32[16,8,128,128]{3,1,2,0:T(8,128)} copy(s32[16,8,128,128]{3,2,1,0:T(8,128)S(1)} %bitcast.310) | data formatting | bytes 16777216
  247.4 11.0 %all-to-all-done.4 = f32[4,8,16,1024]{3,1,0,2:T(8,128)} async-done(((f32[4,8,16,1024]{3,1,0,2:T(8,128)}), f32[4,8,16,1024]{3,1,0,2:T(8,128)}, u32[]{:S(2)}, u32[]{:S(2)}) %all-to-all-start.4) | async-done | bytes 2097184 | tf_op jit(solution)/shard_map/all_to_all | solution.py:89
  258.4 4.5 all-to-all-start.3
  271.7 38.9 %all-to-all-done.3 = f32[4,128,1,1024]{3,0,2,1:T(4,128)} async-done(((f32[4,128,1,1024]{3,0,2,1:T(4,128)}), f32[4,128,1,1024]{3,0,2,1:T(4,128)}, u32[]{:S(2)}, u32[]{:S(2)}) %all-to-all-start.3) | async-done | bytes 2097184 | tf_op jit(solution)/shard_map/all_to_all | solution.py:102
  310.5 4.7 all-to-all-start.2
  338.3 24.1 %all-to-all-done.2 = f32[4,128,1,1024]{3,0,2,1:T(4,128)} async-done(((f32[4,128,1,1024]{3,0,2,1:T(4,128)}), f32[4,128,1,1024]{3,0,2,1:T(4,128)}, u32[]{:S(2)}, u32[]{:S(2)}) %all-to-all-start.2) | async-done | bytes 2097184 | tf_op jit(solution)/shard_map/all_to_all | solution.py:101
  362.4 4.6 all-to-all-start.7
  375.8 38.5 %all-to-all-done.7 = f32[4,128,1,1024]{3,0,2,1:T(4,128)} async-done(((f32[4,128,1,1024]{3,0,2,1:T(4,128)}), f32[4,128,1,1024]{3,0,2,1:T(4,128)}, u32[]{:S(2)}, u32[]{:S(2)}) %all-to-all-start.7) | async-done | bytes 2097184 | tf_op jit(solution)/shard_map/all_to_all | solution.py:102
  414.3 4.7 all-to-all-start.6
  419.8 4.2 copy.146
  425.7 4.2 copy.147
  432.7 4.1 copy.144
  461.2 4.9 all-to-all-done.6
  (114 shorter events, 175.3 us)
Async XLA Ops:
  6.5 19.5 %all-gather.3.cloned.1.call-start = ((), (), s32[]{:S(2)}) async-start(), calls=%async_computation.8 | async-start | bytes 1572864 | tf_op jit(solution)/shard_map/all_gather | solution.py:12
  13.1 14.4 %copy-start = (f32[4,8,128,128]{3,2,1,0:T(8,128)S(1)}, f32[4,8,128,128]{3,2,1,0:T(8,128)}, u32[]{:S(2)}) copy-start(f32[4,8,128,128]{3,2,1,0:T(8,128)} %param.2) | copy-start | bytes 6291460
  31.7 2.2 copy-start.3
  44.3 55.6 %all-to-all-start.1 = ((f32[4,8,16,1024]{3,1,0,2:T(8,128)}), f32[4,8,16,1024]{3,1,0,2:T(8,128)}, u32[]{:S(2)}, u32[]{:S(2)}) async-start(f32[4,8,16,1024]{3,1,0,2:T(8,128)} %copy.33), calls=%async_computation.1 | async-start | bytes 4194304 | tf_op jit(solution)/shard_map/all_to_all | solution.py:92
  51.7 3.9 copy-start.4
  99.9 53.3 %all-to-all-start = ((f32[4,8,16,1024]{3,1,0,2:T(8,128)}), f32[4,8,16,1024]{3,1,0,2:T(8,128)}, u32[]{:S(2)}, u32[]{:S(2)}) async-start(f32[4,8,16,1024]{3,1,0,2:T(8,128)} %copy.31), calls=%async_computation | async-start | bytes 4194304 | tf_op jit(solution)/shard_map/all_to_all | solution.py:89
  105.4 12.6 %all-gather.5.cloned.1.call-start = ((), (), s32[]{:S(2)}) async-start(), calls=%async_computation.9 | async-start | bytes 1572864 | tf_op jit(solution)/shard_map/all_gather | solution.py:12
  119.3 5.7 %copy-start.17 = (f32[8,128,128]{2,1,0:T(8,128)}, f32[8,128,128]{2,1,0:T(8,128)S(1)}, u32[]{:S(2)}) copy-start(f32[8,128,128]{2,1,0:T(8,128)S(1)} %reduce_sum.19) | copy-start | bytes 1572868
  136.3 22.2 %copy-start.6 = (f32[4,8,128,128]{3,2,1,0:T(8,128)S(1)}, f32[4,8,128,128]{3,2,1,0:T(8,128)}, u32[]{:S(2)}) copy-start(f32[4,8,128,128]{3,2,1,0:T(8,128)} %copy-done.5) | copy-start | bytes 6291460
  153.2 52.8 %all-to-all-start.5 = ((f32[4,8,16,1024]{3,1,0,2:T(8,128)}), f32[4,8,16,1024]{3,1,0,2:T(8,128)}, u32[]{:S(2)}, u32[]{:S(2)}) async-start(f32[4,8,16,1024]{3,1,0,2:T(8,128)} %copy.49), calls=%async_computation.5 | async-start | bytes 4194304 | tf_op jit(solution)/shard_map/all_to_all | solution.py:92
  158.5 2.2 copy-start.2
  205.9 52.5 %all-to-all-start.4 = ((f32[4,8,16,1024]{3,1,0,2:T(8,128)}), f32[4,8,16,1024]{3,1,0,2:T(8,128)}, u32[]{:S(2)}, u32[]{:S(2)}) async-start(f32[4,8,16,1024]{3,1,0,2:T(8,128)} %copy.47), calls=%async_computation.4 | async-start | bytes 4194304 | tf_op jit(solution)/shard_map/all_to_all | solution.py:89
  232.0 2.7 copy-start.9
  258.4 52.1 %all-to-all-start.3 = ((f32[4,128,1,1024]{3,0,2,1:T(4,128)}), f32[4,128,1,1024]{3,0,2,1:T(4,128)}, u32[]{:S(2)}, u32[]{:S(2)}) async-start(f32[4,128,1,1024]{3,0,2,1:T(4,128)} %copy.42), calls=%async_computation.3 | async-start | bytes 4194304 | tf_op jit(solution)/shard_map/all_to_all | solution.py:102
  310.5 51.9 %all-to-all-start.2 = ((f32[4,128,1,1024]{3,0,2,1:T(4,128)}), f32[4,128,1,1024]{3,0,2,1:T(4,128)}, u32[]{:S(2)}, u32[]{:S(2)}) async-start(f32[4,128,1,1024]{3,0,2,1:T(4,128)} %copy.37), calls=%async_computation.2 | async-start | bytes 4194304 | tf_op jit(solution)/shard_map/all_to_all | solution.py:101
  322.9 2.2 copy-start.8
  362.4 51.8 %all-to-all-start.7 = ((f32[4,128,1,1024]{3,0,2,1:T(4,128)}), f32[4,128,1,1024]{3,0,2,1:T(4,128)}, u32[]{:S(2)}, u32[]{:S(2)}) async-start(f32[4,128,1,1024]{3,0,2,1:T(4,128)} %copy.58), calls=%async_computation.7 | async-start | bytes 4194304 | tf_op jit(solution)/shard_map/all_to_all | solution.py:102
  375.8 43.2 %copy-start.18 = (f32[8,128,128]{2,1,0:T(8,128)S(1)}, f32[8,128,128]{2,1,0:T(8,128)}, u32[]{:S(2)}) copy-start(f32[8,128,128]{2,1,0:T(8,128)} %copy-done.17) | copy-start | bytes 1572868
  414.3 51.9 %all-to-all-start.6 = ((f32[4,128,1,1024]{3,0,2,1:T(4,128)}), f32[4,128,1,1024]{3,0,2,1:T(4,128)}, u32[]{:S(2)}, u32[]{:S(2)}) async-start(f32[4,128,1,1024]{3,0,2,1:T(4,128)} %copy.53), calls=%async_computation.6 | async-start | bytes 4194304 | tf_op jit(solution)/shard_map/all_to_all | solution.py:101
  443.3 3.5 copy-start.10
  450.4 3.6 copy-start.11
  474.5 2.3 copy-start.13
  474.5 2.3 copy-start.16
  476.7 2.2 copy-start.14
  (7 other events, 13.7 us)
Sparse Core Ops, SparseCore 0:
  15.6 10.3 all-gather.2
  107.7 10.1 all-gather.4
